TPU v7x, 256 devices: a whole 4x4x8 slice. The times are simulated.
256 devices in a mesh: row: 8 (over x, z_lo), col: 32 (over y, z_hi, core).
Axes of the slice: x: 4, y: 4, z: 8 (z_hi: 4, z_lo: 2; z = z_hi * 2 + z_lo), core: 2. Of those that a mesh axis runs over, the one named last changes fastest.
Arguments:
- activations: bfloat16 [1024, 8192], P('col', 'row'), may hold values from -6 to 6
- up_weight: bfloat16 [8192, 53248], P('row', 'col'), may hold values from -0.0625 to 0.0625
- out_grad: bfloat16 [1024, 53248], P('row', 'col'), may hold values from -6 to 6
- round_seed: int32 [1], replicated, may hold values from 0 to 1073741823
- counter_base: int32 [1024], P('row'), may hold values from 0 to 1073741823
Outputs:
- weight_grad: float32 [8192, 53248], P('row', 'col')
- input_grad: bfloat16 [1024, 8192], P('col', 'row')
All inputs are finite; a program needn't handle non-finite values.
Results may differ from a plain program's by a relative error of at most 0.015.
Values may be sent and summed in bfloat16 or wider, within the bound.
A program may use at most 64 MiB of HBM per device.

v0:
```python
import jax
import jax.numpy as jnp
from jax import lax
from jax.sharding import PartitionSpec as P


def stochastic_round(grad, counter_base, round_seed, col_first):
    columns = col_first + lax.broadcasted_iota(jnp.int32, grad.shape, 1)
    counter = counter_base[:, None] + columns
    mixed = counter * jnp.int32(747796405) + round_seed[0] * jnp.int32(1013904223)
    mixed = mixed ^ mixed >> 15
    mixed = mixed * jnp.int32(277803737)
    mixed = mixed ^ mixed >> 16
    level = (mixed & 255).astype(jnp.float32)
    scaled = grad.astype(jnp.float32) * 4.0 + (level + 0.5) / 256.0
    return (jnp.floor(scaled) / 4.0).astype(jnp.bfloat16)


def contract(left, right):
    return lax.dot_general(
        left, right, (((0,), (0,)), ((), ())), preferred_element_type=jnp.float32
    )


def project(grad_rows, weight):
    return lax.dot_general(
        grad_rows, weight, (((1,), (1,)), ((), ())), preferred_element_type=jnp.float32
    )


def fold_panels(activations, combine, initial):
    everyone = lax.all_gather(activations, "col", axis=0, tiled=True)
    return combine(initial, everyone, 0)


def shards(activations, up_weight, out_grad, round_seed, counter_base):
    ff_local = out_grad.shape[1]
    d_local = activations.shape[1]
    col_first = lax.axis_index("col") * ff_local
    quantized = stochastic_round(out_grad, counter_base, round_seed, col_first)
    total_tokens = activations.shape[0] * lax.axis_size("col")
    scaling = total_tokens ** (-0.5)
    grad_zero = jnp.zeros((d_local, ff_local), jnp.float32)
    everything = lax.all_gather(quantized, "row", axis=0, tiled=True)

    def accumulate(total, panel, offset):
        return contract(panel, everything)

    weight_grad = fold_panels(activations, accumulate, grad_zero)
    input_grad = lax.psum_scatter(
        project(everything, up_weight).astype(jnp.bfloat16), "col", scatter_dimension=0, tiled=True
    )
    return (weight_grad * scaling, input_grad)


def solution(mesh):
    placed = (P("col", "row"), P("row", "col"), P("row", "col"), P(), P("row"))
    return jax.shard_map(
        shards,
        mesh=mesh,
        in_specs=placed,
        out_specs=(P("row", "col"), P("col", "row")),
        check_vma=False,
    )
```

profile of v0, /device:TPU:36, one launch (start us, length us, event | category | flops | bytes accessed | tf_op | source)
XLA Modules:
  0.0 247.7 jit_solution(7704462598015921384)
XLA Ops:
  7.2 0.0 copy-start
  7.2 0.0 all-gather.3.cloned.1.call-start
  8.0 2.5 %fusion.8 = bf16[128,1664]{1,0:T(8,128)(2,1)} fusion(bf16[128,1664]{1,0:T(8,128)(2,1)} %param.7, s32[]{:T(128)} %bitcast, s32[1664]{0:T(1024)S(1)} %iota_add_fusion, s32[128]{0:T(128)} %param.9), kind=kLoop, calls=%fused_computation.12 | loop fusion | flops 3833856 | bytes 859140 | tf_op jit(solution)/shard_map/convert_element_type | solution.py:16
  10.5 0.0 all-gather.3.cloned.1.call-update
  10.5 0.0 all-gather.5.cloned.1.call-start
  10.6 0.7 all-gather.5.cloned.1.call-update
  11.3 0.0 reduce-scatter.2.cloned.1.call-start
  11.3 79.0 %all-gather.3.cloned.1.call-done = bf16[1024,1664]{1,0:T(8,128)(2,1)} async-done(((bf16[128,1664]{1,0:T(8,128)(2,1)}), bf16[1024,1664]{1,0:T(8,128)(2,1)}) %all-gather.3.cloned.1.call-update) | async-done | bytes 3407888 | tf_op jit(solution)/shard_map/all_gather | solution.py:44
  90.4 0.0 copy-done
  90.4 7.1 %convolution_convert_fusion = bf16[1024,1024]{1,0:T(8,128)(2,1)} fusion(bf16[1024,1664]{1,0:T(8,128)(2,1)} %all-gather.3.cloned.1.call-done, bf16[1024,1664]{1,0:T(8,128)(2,1)S(1)} %copy-done), kind=kOutput, calls=%fused_computation.1 | convolution fusion | flops 3490709504 | bytes 8912896 | tf_op jit(solution)/shard_map/dot_general | solution.py:26
  97.5 0.0 reduce-scatter.2.cloned.1.call-update
  97.6 49.7 %all-gather.5.cloned.1.call-done = bf16[1024,1024]{1,0:T(8,128)(2,1)} async-done(((bf16[32,1024]{1,0:T(8,128)(2,1)}), bf16[1024,1024]{1,0:T(8,128)(2,1)}) %all-gather.5.cloned.1.call-update) | async-done | bytes 2097168 | tf_op jit(solution)/shard_map/all_gather | solution.py:32
  147.3 9.2 %multiply_bitcast_fusion = f32[1024,1664]{0,1:T(8,128)} fusion(bf16[1024,1664]{1,0:T(8,128)(2,1)} %all-gather.3.cloned.1.call-done, bf16[1024,1024]{1,0:T(8,128)(2,1)} %all-gather.5.cloned.1.call-done), kind=kOutput, calls=%fused_computation | convolution fusion | flops 3491364864 | bytes 12320768 | tf_op jit(solution)/shard_map/dot_general | solution.py:20
  156.4 7.6 %copy.7 = f32[1024,1664]{1,0:T(8,128)} copy(f32[1024,1664]{0,1:T(8,128)} %multiply_bitcast_fusion) | data formatting | bytes 13631488
  164.0 77.1 %reduce-scatter.2.cloned.1.call-done = bf16[32,1024]{1,0:T(8,128)(2,1)} async-done(((bf16[1024,1024]{1,0:T(8,128)(2,1)}), bf16[32,1024]{1,0:T(8,128)(2,1)}) %reduce-scatter.2.cloned.1.call-update) | async-done | bytes 65552 | tf_op jit(solution)/shard_map/reduce_scatter | solution.py:50
  (1 shorter events, 0.0 us)
Async XLA Ops:
  7.2 83.2 %copy-start = (bf16[1024,1664]{1,0:T(8,128)(2,1)S(1)}, bf16[1024,1664]{1,0:T(8,128)(2,1)}, u32[]{:S(2)}) copy-start(bf16[1024,1664]{1,0:T(8,128)(2,1)} %param.6) | copy-start | bytes 10223620
  7.2 83.2 %all-gather.3.cloned.1.call-start = ((), (), s32[]{:S(2)}) async-start(), calls=%async_computation.1 | async-start | bytes 3833856 | tf_op jit(solution)/shard_map/all_gather | solution.py:44
  10.5 136.7 %all-gather.5.cloned.1.call-start = ((), (), s32[]{:S(2)}) async-start(), calls=%async_computation.2 | async-start | bytes 2162688 | tf_op jit(solution)/shard_map/all_gather | solution.py:32
  11.3 229.8 %reduce-scatter.2.cloned.1.call-start = ((), (), s32[]{:S(2)}) async-start(), calls=%async_computation.3 | async-start | bytes 2162688 | tf_op jit(solution)/shard_map/reduce_scatter | solution.py:50
Sparse Core Ops, SparseCore 0:
  10.7 79.6 all-gather.2
  92.9 54.2 all-gather.4
  151.7 89.4 reduce-scatter.1
where the time goes:
time: 249 us; the launch traced here: 248 us
  waiting for transfers between devices  207 us (83%)
  matrix products  16.3 us (7%)
  between operations  14.6 us (6%)
  local copies, waits for them, and re-layouts  7.62 us (3%)
  other arithmetic  2.49 us (1%)
    all_gather x1, waiting for transfers between devices, shards(): everything = lax.all_gather(quantized, 'row', axis=0, tiled=True)  79 us
    reduce_scatter x1, waiting for transfers between devices, shards(): lax.psum_scatter(project(everything, up_weight).astype(jnp.bfloat16), 'co...  77.1 us
    all_gather x1, waiting for transfers between devices, fold_panels(): everyone = lax.all_gather(activations, 'col', axis=0, tiled=True)  49.7 us
    dot_general x1, matrix products, contract(): lax.dot_general(left, right, (((0,), (0,)), ((), ())), preferred_element_...  9.16 us
    unnamed x3, local copies, waits for them, and re-layouts  7.62 us
    dot_general x1, matrix products, project(): lax.dot_general(grad_rows, weight, (((1,), (1,)), ((), ())), preferred_el...  7.14 us
  transfers between devices with their start and end apart: 3, of which 3 were waited for; matrix products, arithmetic and copies ran while one was open for 10% of the time, Pallas kernels for 0%

commit v1 on v0

v1 whole, which is shorter than its diff:
```python
import functools

import jax
import jax.numpy as jnp
from jax import lax
from jax.experimental import pallas as pl
from jax.experimental.pallas import tpu as pltpu
from jax.sharding import PartitionSpec as P

MESH = pl.DeviceIdType.MESH
NX, NY, NH = 4, 4, 4
OWN, LEFT, RIGHT, FAR, OWN2, LEFT2, RIGHT2, FAR2 = range(8)
SHARDS = ((0, 0), (3, 0), (1, 0), (2, 0), (0, 1), (3, 1), (1, 1), (2, 1))


def place():
    row, col = lax.axis_index("row"), lax.axis_index("col")
    return lax.div(row, 2), lax.rem(row, 2), lax.div(col, 8), lax.rem(lax.div(col, 2), 4), lax.rem(col, 2)


def device(x, lo, y, hi, core):
    return (x * 2 + lo, (y * NH + hi) * 2 + core)


def exchange_kernel(
    act_hbm, weight_hbm, grad_hbm, seed_ref, base_ref, g_ref, a_ref, out_ref,
    grad, weight, part, crecv, ssum, yrecv, tsum, zrecv,
    lsem, gs, gr, cs, cr, ys, yr, zs, zr, azs, azr, ays, ayr, acs, acr,
):
    x, lo, y, hi, core = place()
    tokens, ff = grad.shape
    block = tokens // 4
    my_slot = x * 2 + lo
    here = device(x, lo, y, hi, core)
    right = device(lax.rem(x + 1, NX), lo, y, hi, core)
    left = device(lax.rem(x + 3, NX), lo, y, hi, core)
    pair = device(x, 1 - lo, y, hi, core)
    sibling = device(x, lo, y, hi, 1 - core)

    def at_y(yy):
        return device(x, lo, yy, hi, core)

    def at_hi(hh):
        return device(x, lo, y, hh, core)

    def slot(i):
        dx, other = SHARDS[i]
        return lax.rem(x + dx, NX) * 2 + lax.rem(lo + other, 2)

    load_grad = pltpu.make_async_copy(grad_hbm, grad, lsem.at[0])
    load_grad.start()
    load_weight = pltpu.make_async_copy(weight_hbm, weight, lsem.at[1])
    load_weight.start()
    load_act = pltpu.make_async_copy(act_hbm, a_ref.at[y, hi, core], lsem.at[2])
    load_act.start()

    barrier = pltpu.get_barrier_semaphore()
    peers = [right, left, pair, sibling]
    peers += [at_y(lax.rem(y + d, NY)) for d in (1, 2, 3)]
    peers += [at_hi(lax.rem(hi + d, NH)) for d in (1, 2, 3)]
    for peer in peers:
        pl.semaphore_signal(barrier, inc=1, device_id=peer, device_id_type=MESH)

    load_grad.wait()
    base = jnp.transpose(jnp.broadcast_to(base_ref[...], (tokens, tokens)))
    mixed_seed = seed_ref[0] * jnp.int32(1013904223)
    first = lax.axis_index("col") * ff

    def round_columns(n, _):
        columns = pl.ds(pl.multiple_of(n * 128, 128), 128)
        counter = base + (first + n * 128 + lax.broadcasted_iota(jnp.int32, (tokens, 128), 1))
        mixed = counter * jnp.int32(747796405) + mixed_seed
        mixed = mixed ^ (mixed >> 15)
        mixed = mixed * jnp.int32(277803737)
        mixed = mixed ^ (mixed >> 16)
        level = (mixed & 255).astype(jnp.float32)
        scaled = grad[:, columns].astype(jnp.float32) * 4.0 + (level + 0.5) / 256.0
        rounded = (jnp.floor(scaled) / 4.0).astype(jnp.bfloat16)
        g_ref[my_slot, :, :, columns] = rounded.reshape(4, block, 128)
        return 0

    lax.fori_loop(0, ff // 128, round_columns, 0)
    pl.semaphore_wait(barrier, len(peers))

    sends = []

    def send_g(i, j, to):
        where = g_ref.at[slot(i), j]
        copy = pltpu.make_async_remote_copy(
            src_ref=where, dst_ref=where, send_sem=gs.at[len(sends)], recv_sem=gr.at[slot(i), j],
            device_id=to, device_id_type=MESH,
        )
        copy.start()
        sends.append(copy)

    def wait_g(i, *js):
        for j in js:
            where = g_ref.at[slot(i), j]
            pltpu.make_async_remote_copy(
                src_ref=where, dst_ref=where, send_sem=gs.at[0], recv_sem=gr.at[slot(i), j],
                device_id=here, device_id_type=MESH,
            ).wait_recv()

    def core_copy(i):
        return pltpu.make_async_remote_copy(
            src_ref=part.at[i, :, 1 - core], dst_ref=crecv.at[i], send_sem=cs.at[i], recv_sem=cr.at[i],
            device_id=sibling, device_id_type=MESH,
        )

    def project(i):
        where = slot(i)

        def features(n, _):
            wide = pl.ds(pl.multiple_of(n * 256, 256), 256)
            value = lax.dot_general(
                g_ref[where].reshape(tokens, ff), weight[wide, :], (((1,), (1,)), ((), ())),
                preferred_element_type=jnp.float32,
            )
            part[i, :, :, :, wide] = value.astype(jnp.bfloat16).reshape(2, 2, block, 256)
            return 0

        lax.fori_loop(0, weight.shape[0] // 256, features, 0)
        core_copy(i).start()

    def root(i):
        return lax.rem(x + SHARDS[i][0], NX)

    def y_copy(i):
        to = root(i)
        lo_root = lax.rem(lo + SHARDS[i][1], 2)
        k = lax.rem(y + NY - to, NY) - 1
        return pltpu.make_async_remote_copy(
            src_ref=ssum.at[i], dst_ref=yrecv.at[lo_root, k], send_sem=ys.at[i], recv_sem=yr.at[lo_root, k],
            device_id=at_y(to), device_id_type=MESH,
        )

    def add_cores(i):
        core_copy(i).wait_recv()
        ssum[i] = (part[i, :, core].astype(jnp.float32) + crecv[i].astype(jnp.float32)).astype(jnp.bfloat16)

        @pl.when(y != root(i))
        def _():
            y_copy(i).start()

    def z_copy(lo_root, q):
        to = 2 * lo_root + q
        k = lax.rem(hi + NH - to, NH) - 1
        return pltpu.make_async_remote_copy(
            src_ref=tsum.at[lo_root, q], dst_ref=zrecv.at[k], send_sem=zs.at[lo_root, q], recv_sem=zr.at[k],
            device_id=at_hi(to), device_id_type=MESH,
        )

    def add_columns(i):
        @pl.when(y == root(i))
        def _():
            lo_root = lax.rem(lo + SHARDS[i][1], 2)
            total = ssum[i].astype(jnp.float32)
            for k in range(3):
                pltpu.make_async_remote_copy(
                    src_ref=ssum.at[i], dst_ref=yrecv.at[lo_root, k], send_sem=ys.at[i], recv_sem=yr.at[lo_root, k],
                    device_id=here, device_id_type=MESH,
                ).wait_recv()
                total += yrecv[lo_root, k].astype(jnp.float32)
            tsum[lo_root] = total.astype(jnp.bfloat16)
            for q in range(2):

                @pl.when(hi != 2 * lo_root + q)
                def _():
                    z_copy(lo_root, q).start()

    def az_copy(d):
        where = a_ref.at[y, hi, core]
        return pltpu.make_async_remote_copy(
            src_ref=where, dst_ref=where, send_sem=azs.at[d - 1], recv_sem=azr.at[d - 1],
            device_id=at_hi(lax.rem(hi + d, NH)), device_id_type=MESH,
        )

    def ay_copy(d):
        where = a_ref.at[y, :, core]
        return pltpu.make_async_remote_copy(
            src_ref=where, dst_ref=where, send_sem=ays.at[d - 1], recv_sem=ayr.at[d - 1],
            device_id=at_y(lax.rem(y + d, NY)), device_id_type=MESH,
        )

    def ac_copy(d):
        where = a_ref.at[lax.rem(y + NY - d, NY), :, core]
        return pltpu.make_async_remote_copy(
            src_ref=where, dst_ref=where, send_sem=acs.at[d], recv_sem=acr.at[d],
            device_id=sibling, device_id_type=MESH,
        )

    def az_wait(d):
        where = a_ref.at[y, lax.rem(hi + NH - d, NH), core]
        pltpu.make_async_remote_copy(
            src_ref=where, dst_ref=where, send_sem=azs.at[d - 1], recv_sem=azr.at[d - 1],
            device_id=here, device_id_type=MESH,
        ).wait_recv()

    def ay_wait(d):
        where = a_ref.at[lax.rem(y + NY - d, NY), :, core]
        pltpu.make_async_remote_copy(
            src_ref=where, dst_ref=where, send_sem=ays.at[d - 1], recv_sem=ayr.at[d - 1],
            device_id=here, device_id_type=MESH,
        ).wait_recv()

    def ac_wait(d):
        where = a_ref.at[lax.rem(y + NY - d, NY), :, 1 - core]
        pltpu.make_async_remote_copy(
            src_ref=where, dst_ref=where, send_sem=acs.at[d], recv_sem=acr.at[d],
            device_id=here, device_id_type=MESH,
        ).wait_recv()

    for j, k, p in ((0, 3, 0), (1, 2, 3), (2, 1, 1), (3, 0, 2)):
        send_g(OWN, j, right)
        send_g(OWN, k, left)
        send_g(OWN, p, pair)
    load_weight.wait()
    project(OWN)
    wait_g(LEFT, 0)
    send_g(LEFT, 0, right)
    wait_g(RIGHT, 3)
    send_g(RIGHT, 3, left)
    add_cores(OWN)
    wait_g(LEFT, 1)
    send_g(LEFT, 1, right)
    wait_g(RIGHT, 2)
    send_g(RIGHT, 2, left)
    wait_g(OWN2, 0)
    send_g(OWN2, 0, right)
    wait_g(OWN2, 3)
    send_g(OWN2, 3, left)
    wait_g(OWN2, 1)
    send_g(OWN2, 1, right)
    wait_g(OWN2, 2)
    send_g(OWN2, 2, left)
    for j, k in ((2, 1), (3, 0)):
        send_g(OWN2, j, right)
        send_g(OWN2, k, left)
    load_act.wait()
    for d in (1, 2, 3):
        az_copy(d).start()
    wait_g(LEFT, 2, 3)
    project(LEFT)
    wait_g(RIGHT, 1, 0)
    project(RIGHT)
    project(OWN2)
    add_columns(OWN)
    add_cores(LEFT)
    add_cores(RIGHT)
    add_cores(OWN2)
    for d in (1, 2, 3):
        az_wait(d)
    for d in (1, 2, 3):
        ay_copy(d).start()
    ac_copy(0).start()
    wait_g(FAR, 0, 3, 1, 2)
    project(FAR)
    add_columns(LEFT)
    add_columns(RIGHT)
    add_columns(OWN2)
    add_cores(FAR)
    wait_g(LEFT2, 0)
    send_g(LEFT2, 0, right)
    wait_g(RIGHT2, 3)
    send_g(RIGHT2, 3, left)
    wait_g(LEFT2, 1)
    send_g(LEFT2, 1, right)
    wait_g(RIGHT2, 2)
    send_g(RIGHT2, 2, left)
    add_columns(FAR)
    for d in (1, 2, 3):
        ay_wait(d)
        ac_copy(d).start()
    wait_g(LEFT2, 2, 3)
    project(LEFT2)
    wait_g(RIGHT2, 1, 0)
    project(RIGHT2)
    add_cores(LEFT2)
    add_cores(RIGHT2)
    wait_g(FAR2, 0, 3, 1, 2)
    project(FAR2)
    add_columns(LEFT2)
    add_columns(RIGHT2)
    add_cores(FAR2)
    add_columns(FAR2)
    for d in range(4):
        ac_wait(d)

    own_lo, own_q = lax.div(hi, 2), lax.rem(hi, 2)
    total = tsum[own_lo, own_q].astype(jnp.float32)
    for k in range(3):
        pltpu.make_async_remote_copy(
            src_ref=zrecv.at[k], dst_ref=zrecv.at[k], send_sem=zs.at[0, 0], recv_sem=zr.at[k],
            device_id=here, device_id_type=MESH,
        ).wait_recv()
        total += zrecv[k].astype(jnp.float32)
    out_ref[...] = total.astype(jnp.bfloat16)

    for copy in sends:
        copy.wait_send()
    for i in range(8):
        core_copy(i).wait_send()

        @pl.when(y != root(i))
        def _():
            y_copy(i).wait_send()

        @pl.when(y == root(i))
        def _():
            lo_root = lax.rem(lo + SHARDS[i][1], 2)
            for q in range(2):

                @pl.when(hi != 2 * lo_root + q)
                def _():
                    z_copy(lo_root, q).wait_send()

    for d in (1, 2, 3):
        az_copy(d).wait_send()
        ay_copy(d).wait_send()
    for d in range(4):
        ac_copy(d).wait_send()


def shards(activations, up_weight, out_grad, round_seed, counter_base):
    tokens, ff = out_grad.shape
    few, features = activations.shape
    all_tokens = few * lax.axis_size("col")
    bf16, dma = jnp.bfloat16, pltpu.SemaphoreType.DMA
    vmem, anywhere = pl.BlockSpec(memory_space=pltpu.VMEM), pl.BlockSpec(memory_space=pl.ANY)
    g, a, input_grad = pl.pallas_call(
        exchange_kernel,
        out_shape=(
            pltpu.VMEM((8, 4, tokens // 4, ff), bf16),
            pltpu.VMEM((NY, NH, 2, few, features), bf16),
            jax.ShapeDtypeStruct((few, features), bf16),
        ),
        in_specs=[anywhere, anywhere, anywhere, pl.BlockSpec(memory_space=pltpu.SMEM), vmem],
        out_specs=(vmem, vmem, vmem),
        scratch_shapes=[
            pltpu.VMEM((tokens, ff), bf16),
            pltpu.VMEM((features, ff), bf16),
            pltpu.VMEM((8, 2, 2, few, features), bf16),
            pltpu.VMEM((8, 2, few, features), bf16),
            pltpu.VMEM((8, 2, few, features), bf16),
            pltpu.VMEM((2, 3, 2, few, features), bf16),
            pltpu.VMEM((2, 2, few, features), bf16),
            pltpu.VMEM((3, few, features), bf16),
            dma((3,)), dma((28,)), dma((8, 4)), dma((8,)), dma((8,)), dma((8,)), dma((2, 3)),
            dma((2, 2)), dma((3,)), dma((3,)), dma((3,)), dma((3,)), dma((3,)), dma((4,)), dma((4,)),
        ],
        compiler_params=pltpu.CompilerParams(
            collective_id=0, has_side_effects=True, vmem_limit_bytes=48 * 1024 * 1024
        ),
        name="exchange",
    )(activations, up_weight, out_grad, round_seed, counter_base.reshape(1, tokens))
    weight_grad = lax.dot_general(
        a.reshape(all_tokens, features), g.reshape(all_tokens, ff), (((0,), (0,)), ((), ())),
        preferred_element_type=jnp.float32,
    )
    return weight_grad * all_tokens ** (-0.5), input_grad


def solution(mesh):
    placed = (P("col", "row"), P("row", "col"), P("row", "col"), P(), P("row"))
    return jax.shard_map(
        shards,
        mesh=mesh,
        in_specs=placed,
        out_specs=(P("row", "col"), P("col", "row")),
        check_vma=False,
    )
```

time: 249 us -> 80.1 us (0.32)
  waiting for transfers between devices: 207 us -> 0 us
  Pallas kernels: 0 us -> 69.3 us
  between operations: 14.6 us -> 1.3 us
  matrix products: 16.3 us -> 6.15 us
  local copies, waits for them, and re-layouts: 7.62 us -> 3.12 us
  other arithmetic: 2.49 us -> 0 us
    all_gather x2 -> x0, waiting for transfers between devices: 129 us -> none  [the longest x1 79 us: shards(): everything = lax.all_gather(quantized, 'row', axis=0, tiled=True)]
    reduce_scatter x1 -> x0, waiting for transfers between devices: 77.1 us -> none  [shards(): lax.psum_scatter(project(everything, up_weight).astype(jnp.bfloat16), 'co...]
    pallas_call x0 -> x1, Pallas kernels: none -> 69.3 us  [shards(): pl.pallas_call(exchange_kernel, out_shape=(pltpu.VMEM((8, 4, tokens // 4,...]
    dot_general x2 -> x1, matrix products: 16.3 us -> 6.15 us  [shards(): lax.dot_general(a.reshape(all_tokens, features), g.reshape(all_tokens, ff...]
    unnamed x3 -> x7, local copies, waits for them, and re-layouts: 7.62 us -> 3.12 us
  transfers between devices with their start and end apart: 3 -> 0, of which waited for: 3 -> 0; matrix products, arithmetic and copies ran while one was open for 10% -> 0% of each run, Pallas kernels for 0% -> 0%
where the time goes in v1:
time: 80.1 us; the launch traced here: 79.9 us
  Pallas kernels  69.3 us (87%)
  matrix products  6.15 us (8%)
  local copies, waits for them, and re-layouts  3.12 us (4%)
  between operations  1.3 us (2%)
    pallas_call x1, Pallas kernels, shards(): pl.pallas_call(exchange_kernel, out_shape=(pltpu.VMEM((8, 4, tokens // 4,...  69.3 us
    dot_general x1, matrix products, shards(): lax.dot_general(a.reshape(all_tokens, features), g.reshape(all_tokens, ff...  6.15 us
    unnamed x7, local copies, waits for them, and re-layouts  3.12 us

profile of v1, /device:TPU:36, one launch (start us, length us, event | category | flops | bytes accessed | tf_op | source)
XLA Modules:
  0.0 79.9 jit_solution(15336803963301648023)
XLA Ops:
  1.3 0.0 copy-start
  1.3 1.0 %copy-done = bf16[128,1664]{1,0:T(8,128)(2,1)S(1)} copy-done((bf16[128,1664]{1,0:T(8,128)(2,1)S(1)}, bf16[128,1664]{1,0:T(8,128)(2,1)}, u32[]{:S(2)}) %copy-start) | copy-done | bytes 426008
  2.3 0.0 copy-start.1
  2.3 0.8 %copy-done.1 = bf16[32,1024]{1,0:T(8,128)(2,1)S(1)} copy-done((bf16[32,1024]{1,0:T(8,128)(2,1)S(1)}, bf16[32,1024]{1,0:T(8,128)(2,1)}, u32[]{:S(2)}) %copy-start.1) | copy-done | bytes 65560
  3.1 0.0 copy-start.2
  3.1 0.7 copy-done.2
  3.8 69.3 %exchange.1 = (bf16[8,4,32,1664]{3,2,1,0:T(8,128)(2,1)S(1)}, bf16[4,4,2,32,1024]{4,3,2,1,0:T(8,128)(2,1)S(1)}, bf16[32,1024]{1,0:T(8,128)(2,1)S(1)}) custom-call(bf16[32,1024]{1,0:T(8,128)(2,1)S(1)} %copy-done.1, bf16[1024,1664]{1,0:T(8,128)(2,1)} %weight_hbm.1, bf16[128,1664]{1,0:T(8,128)(2,1)S(1)} %copy-done, s32[1]{0:T(128)S(6)} %copy.8.seed_ref, ...), custom_call_target="tpu_custom_call" | custom-call | tf_op jit(solution)/shard_map/exchange/pallas_call | solution.py:330
  73.1 6.2 %convolution_multiply_fusion = f32[1024,1664]{1,0:T(8,128)} fusion(bf16[1024,1024]{1,0:T(8,128)(2,1)S(1)} %bitcast.7, bf16[1024,1664]{1,0:T(8,128)(2,1)S(1)} %bitcast.6), kind=kOutput, calls=%fused_computation | convolution fusion | flops 3491364864 | bytes 12320768 | tf_op jit(solution)/shard_map/dot_general | solution.py:356
  79.2 0.6 copy.9
Async XLA Ops:
  1.3 1.0 %copy-start = (bf16[128,1664]{1,0:T(8,128)(2,1)S(1)}, bf16[128,1664]{1,0:T(8,128)(2,1)}, u32[]{:S(2)}) copy-start(bf16[128,1664]{1,0:T(8,128)(2,1)} %grad_hbm.1) | copy-start | bytes 1277956
  2.3 0.8 %copy-start.1 = (bf16[32,1024]{1,0:T(8,128)(2,1)S(1)}, bf16[32,1024]{1,0:T(8,128)(2,1)}, u32[]{:S(2)}) copy-start(bf16[32,1024]{1,0:T(8,128)(2,1)} %act_hbm.1) | copy-start | bytes 196612
  3.1 0.7 copy-start.2

commit v2 on v0

v2 whole, which is shorter than its diff:
```python
import jax
import jax.numpy as jnp
from jax import lax
from jax.experimental import pallas as pl
from jax.experimental.pallas import tpu as pltpu
from jax.sharding import PartitionSpec as P

MESH = pl.DeviceIdType.MESH
NX, NY, NH = 4, 4, 4
OWN, LEFT, RIGHT, FAR, OWN2, LEFT2, RIGHT2, FAR2 = range(8)
SHARDS = ((0, 0), (3, 0), (1, 0), (2, 0), (0, 1), (3, 1), (1, 1), (2, 1))
WIDE = 512


def device(x, lo, y, hi, core):
    return (x * 2 + lo, (y * NH + hi) * 2 + core)


def exchange_kernel(
    act_hbm, weight_hbm, grad_hbm, base_hbm, seed_ref, total_ref, out_ref,
    g_ref, a_ref, grad, weight, turned, turned_act, base_row, part, crecv, ssum, yrecv, tsum, zrecv,
    lsem, gs, gr, cs, cr, ys, yr, zs, zr, azs, azr, ays, ayr, acs, acr,
):
    row, col = lax.axis_index("row"), lax.axis_index("col")
    x, lo = lax.div(row, 2), lax.rem(row, 2)
    y, hi, core = lax.div(col, 8), lax.rem(lax.div(col, 2), 4), lax.rem(col, 2)
    tokens, ff = grad.shape
    features = weight.shape[0]
    block = tokens // 4
    here = device(x, lo, y, hi, core)
    right = device(lax.rem(x + 1, NX), lo, y, hi, core)
    left = device(lax.rem(x + 3, NX), lo, y, hi, core)
    pair = device(x, 1 - lo, y, hi, core)
    sibling = device(x, lo, y, hi, 1 - core)

    def at_y(yy):
        return device(x, lo, yy, hi, core)

    def at_hi(hh):
        return device(x, lo, y, hh, core)

    def lo_of(i):
        return lax.rem(lo + SHARDS[i][1], 2)

    def root(i):
        return lax.rem(x + SHARDS[i][0], NX)

    def slot(i):
        return root(i) * 2 + lo_of(i)

    def remote(src, dst, send, recv, to):
        return pltpu.make_async_remote_copy(
            src_ref=src, dst_ref=dst, send_sem=send, recv_sem=recv, device_id=to, device_id_type=MESH
        )

    loads = [
        pltpu.make_async_copy(base_hbm, base_row, lsem.at[0]),
        pltpu.make_async_copy(grad_hbm, grad, lsem.at[1]),
        pltpu.make_async_copy(act_hbm, a_ref.at[y, hi, core], lsem.at[2]),
        pltpu.make_async_copy(weight_hbm, weight, lsem.at[3]),
    ]
    for load in loads:
        load.start()

    barrier = pltpu.get_barrier_semaphore()
    peers = [right, left, pair, sibling]
    peers += [at_y(lax.rem(y + d, NY)) for d in (1, 2, 3)]
    peers += [at_hi(lax.rem(hi + d, NH)) for d in (1, 2, 3)]
    for peer in peers:
        pl.semaphore_signal(barrier, inc=1, device_id=peer, device_id_type=MESH)

    for load in loads[:3]:
        load.wait()
    base = jnp.transpose(jnp.broadcast_to(base_row[...], (tokens, tokens)))
    mixed_seed = seed_ref[0] * jnp.int32(1013904223)
    first = col * ff

    def round_columns(n, _):
        columns = pl.ds(pl.multiple_of(n * 128, 128), 128)
        counter = base + (first + n * 128 + lax.broadcasted_iota(jnp.int32, (tokens, 128), 1))
        mixed = counter * jnp.int32(747796405) + mixed_seed
        mixed = mixed ^ (mixed >> 15)
        mixed = mixed * jnp.int32(277803737)
        mixed = mixed ^ (mixed >> 16)
        level = (mixed & 255).astype(jnp.float32)
        scaled = grad[:, columns].astype(jnp.float32) * 4.0 + (level + 0.5) / 256.0
        rounded = (jnp.floor(scaled) / 4.0).astype(jnp.bfloat16)
        g_ref[slot(OWN), :, :, columns] = rounded.reshape(4, block, 128)
        return 0

    lax.fori_loop(0, ff // 128, round_columns, 0)
    pl.semaphore_wait(barrier, len(peers))

    sends = []

    def send_g(i, j, to):
        where = g_ref.at[slot(i), j]
        copy = remote(where, where, gs.at[len(sends)], gr.at[slot(i), j], to)
        copy.start()
        sends.append(copy)

    def wait_g(i, *js):
        for j in js:
            where = g_ref.at[slot(i), j]
            remote(where, where, gs.at[0], gr.at[slot(i), j], here).wait_recv()

    def core_copy(i, q):
        return remote(part.at[i, q, 1 - core], crecv.at[i, q], cs.at[i, q], cr.at[i, q], sibling)

    def project(*units):
        rows = 2 * block

        def step(n, _):
            wide = pl.ds(pl.multiple_of(n * WIDE, WIDE), WIDE)
            left_side = jnp.concatenate(
                [g_ref[slot(i), pl.ds(2 * q, 2)].reshape(rows, ff) for i, q in units], axis=0
            )
            value = lax.dot_general(
                left_side, turned[:, wide], (((1,), (0,)), ((), ())), preferred_element_type=jnp.float32
            ).astype(jnp.bfloat16)
            for u, (i, q) in enumerate(units):
                part[i, q, :, :, wide] = value[u * rows : (u + 1) * rows].reshape(2, block, WIDE)
            return 0

        lax.fori_loop(0, features // WIDE, step, 0)
        for i, q in units:
            core_copy(i, q).start()

    def y_copy(i, q):
        k = lax.rem(y + NY - root(i), NY) - 1
        return remote(ssum.at[i, q], yrecv.at[lo_of(i), k, q], ys.at[i, q], yr.at[lo_of(i), k, q], at_y(root(i)))

    def add_cores(*units):
        for i, q in units:
            core_copy(i, q).wait_recv()
            ssum[i, q] = (part[i, q, core].astype(jnp.float32) + crecv[i, q].astype(jnp.float32)).astype(jnp.bfloat16)

            @pl.when(y != root(i))
            def _():
                y_copy(i, q).start()

    def z_copy(lo_root, q):
        to = 2 * lo_root + q
        k = lax.rem(hi + NH - to, NH) - 1
        return remote(tsum.at[lo_root, q], zrecv.at[k], zs.at[lo_root, q], zr.at[k], at_hi(to))

    def add_columns(*units):
        for i, q in units:

            @pl.when(y == root(i))
            def _():
                lo_root = lo_of(i)
                total = ssum[i, q].astype(jnp.float32)
                for k in range(3):
                    where = yrecv.at[lo_root, k, q]
                    remote(where, where, ys.at[i, q], yr.at[lo_root, k, q], here).wait_recv()
                    total += yrecv[lo_root, k, q].astype(jnp.float32)
                tsum[lo_root, q] = total.astype(jnp.bfloat16)

                @pl.when(hi != 2 * lo_root + q)
                def _():
                    z_copy(lo_root, q).start()

    def az_copy(d):
        where = a_ref.at[y, hi, core]
        return remote(where, where, azs.at[d - 1], azr.at[d - 1], at_hi(lax.rem(hi + d, NH)))

    def az_wait(d):
        where = a_ref.at[y, lax.rem(hi + NH - d, NH), core]
        remote(where, where, azs.at[d - 1], azr.at[d - 1], here).wait_recv()

    def ay_copy(d):
        where = a_ref.at[y, :, core]
        return remote(where, where, ays.at[d - 1], ayr.at[d - 1], at_y(lax.rem(y + d, NY)))

    def ay_wait(d):
        where = a_ref.at[lax.rem(y + NY - d, NY), :, core]
        remote(where, where, ays.at[d - 1], ayr.at[d - 1], here).wait_recv()

    def ac_copy(d):
        where = a_ref.at[lax.rem(y + NY - d, NY), :, core]
        return remote(where, where, acs.at[d], acr.at[d], sibling)

    def ac_wait(d):
        where = a_ref.at[lax.rem(y + NY - d, NY), :, 1 - core]
        remote(where, where, acs.at[d], acr.at[d], here).wait_recv()

    def turn_act(plane):
        for r in range(NX):
            rows = a_ref[r, pl.ds(2 * plane, 2)].reshape(tokens, features)
            turned_act[:, r * tokens : (r + 1) * tokens] = jnp.transpose(rows)

    def accumulate(plane, lowest, highest, last):
        for r in range(0, features, 256):
            value = jnp.zeros((256, highest - lowest), jnp.float32)
            for k in range(NX):
                value += lax.dot_general(
                    turned_act[r : r + 256, k * tokens : (k + 1) * tokens],
                    g_ref[2 * k + plane, :, :, lowest:highest].reshape(tokens, highest - lowest),
                    (((1,), (0,)), ((), ())),
                    preferred_element_type=jnp.float32,
                )
            if last:
                value = (total_ref[r : r + 256, lowest:highest] + value) * (NX * 2 * tokens) ** (-0.5)
            total_ref[r : r + 256, lowest:highest] = value

    spans = [(n, min(n + 512, ff)) for n in range(0, ff, 512)]

    for d in (1, 2, 3):
        az_copy(d).start()
    for j, k, p in ((0, 3, 0), (1, 2, 3), (2, 1, 1), (3, 0, 2)):
        send_g(OWN, j, right)
        send_g(OWN, k, left)
        send_g(OWN, p, pair)
    loads[3].wait()

    def turn_weight(n, _):
        some = pl.ds(pl.multiple_of(n * 128, 128), 128)
        turned[:, some] = jnp.transpose(weight[some, :])
        return 0

    lax.fori_loop(0, features // 128, turn_weight, 0)
    project((OWN, 0), (OWN, 1))
    wait_g(LEFT, 0)
    send_g(LEFT, 0, right)
    wait_g(RIGHT, 3)
    send_g(RIGHT, 3, left)
    add_cores((OWN, 0), (OWN, 1))
    wait_g(LEFT, 1)
    send_g(LEFT, 1, right)
    wait_g(RIGHT, 2)
    send_g(RIGHT, 2, left)
    for d in (1, 2, 3):
        az_wait(d)
    for d in (1, 2, 3):
        ay_copy(d).start()
    ac_copy(0).start()
    wait_g(OWN2, 0)
    send_g(OWN2, 0, right)
    wait_g(OWN2, 3)
    send_g(OWN2, 3, left)
    wait_g(LEFT, 2, 3)
    wait_g(RIGHT, 1, 0)
    project((LEFT, 0), (LEFT, 1), (RIGHT, 0), (RIGHT, 1))
    wait_g(OWN2, 1)
    send_g(OWN2, 1, right)
    wait_g(OWN2, 2)
    send_g(OWN2, 2, left)
    for j, k in ((2, 1), (3, 0)):
        send_g(OWN2, j, right)
        send_g(OWN2, k, left)
    add_cores((LEFT, 0), (LEFT, 1), (RIGHT, 0), (RIGHT, 1))
    wait_g(FAR, 0, 3)
    send_g(FAR, 0, pair)
    send_g(FAR, 3, pair)
    add_columns((OWN, 0), (OWN, 1))
    wait_g(FAR, 1, 2)
    send_g(FAR, 1, pair)
    send_g(FAR, 2, pair)
    project((OWN2, 0), (OWN2, 1), (FAR, 0), (FAR, 1))
    add_cores((OWN2, 0), (OWN2, 1), (FAR, 0), (FAR, 1))
    for d in (1, 2, 3):
        ay_wait(d)
        ac_copy(d).start()
    add_columns((LEFT, 0), (LEFT, 1), (RIGHT, 0), (RIGHT, 1))
    wait_g(LEFT2, 0, 1)
    wait_g(RIGHT2, 3, 2)
    project((LEFT2, 0), (RIGHT2, 1))
    for d in range(4):
        ac_wait(d)
    add_cores((LEFT2, 0), (RIGHT2, 1))
    turn_act(lo)
    for span in spans:
        accumulate(lo, *span, False)
    add_columns((OWN2, 0), (OWN2, 1), (FAR, 0), (FAR, 1))
    turn_act(1 - lo)
    wait_g(LEFT2, 2, 3)
    wait_g(RIGHT2, 1, 0)
    wait_g(FAR2, 0, 3, 1, 2)
    project((LEFT2, 1), (RIGHT2, 0), (FAR2, 0), (FAR2, 1))
    accumulate(1 - lo, *spans[0], True)
    add_cores((LEFT2, 1), (RIGHT2, 0), (FAR2, 0), (FAR2, 1))
    for span in spans[1:3]:
        accumulate(1 - lo, *span, True)
    add_columns((LEFT2, 0), (RIGHT2, 1), (LEFT2, 1), (RIGHT2, 0), (FAR2, 0), (FAR2, 1))
    for span in spans[3:]:
        accumulate(1 - lo, *span, True)

    total = tsum[lax.div(hi, 2), lax.rem(hi, 2)].astype(jnp.float32)
    for k in range(3):
        remote(zrecv.at[k], zrecv.at[k], zs.at[0, 0], zr.at[k], here).wait_recv()
        total += zrecv[k].astype(jnp.float32)
    out_ref[...] = total.astype(jnp.bfloat16)

    for copy in sends:
        copy.wait_send()
    for i in range(8):
        for q in range(2):
            core_copy(i, q).wait_send()

            @pl.when(y != root(i))
            def _():
                y_copy(i, q).wait_send()

            @pl.when((y == root(i)) & (hi != 2 * lo_of(i) + q))
            def _():
                z_copy(lo_of(i), q).wait_send()

    for d in (1, 2, 3):
        az_copy(d).wait_send()
        ay_copy(d).wait_send()
    for d in range(4):
        ac_copy(d).wait_send()


def store_kernel(total_ref, rows_ref, total_hbm, rows_hbm, sem):
    pieces = 8
    step = total_ref.shape[0] // pieces
    copies = [pltpu.make_async_copy(rows_ref, rows_hbm, sem.at[pieces])]
    for n in range(pieces):
        some = pl.ds(n * step, step)
        copies.append(pltpu.make_async_copy(total_ref.at[some], total_hbm.at[some], sem.at[n]))
    for copy in copies:
        copy.start()
    for copy in copies:
        copy.wait()


def shards(activations, up_weight, out_grad, round_seed, counter_base):
    tokens, ff = out_grad.shape
    few, features = activations.shape
    bf16, f32, dma = jnp.bfloat16, jnp.float32, pltpu.SemaphoreType.DMA
    vmem, hbm = pl.BlockSpec(memory_space=pltpu.VMEM), pl.BlockSpec(memory_space=pltpu.HBM)
    operands = (activations, up_weight, out_grad, counter_base.reshape(1, tokens))
    held = [pltpu.with_memory_space_constraint(v, pltpu.HBM) for v in operands]
    total, input_rows = pl.pallas_call(
        exchange_kernel,
        out_shape=(pltpu.VMEM((features, ff), f32), pltpu.VMEM((few, features), bf16)),
        in_specs=[hbm] * 4 + [pl.BlockSpec(memory_space=pltpu.SMEM)],
        out_specs=(vmem, vmem),
        scratch_shapes=[
            pltpu.VMEM((8, 4, tokens // 4, ff), bf16),
            pltpu.VMEM((NY, NH, 2, few, features), bf16),
            pltpu.VMEM((tokens, ff), bf16),
            pltpu.VMEM((features, ff), bf16),
            pltpu.VMEM((ff, features), bf16),
            pltpu.VMEM((features, NX * tokens), bf16),
            pltpu.VMEM((1, tokens), jnp.int32),
            pltpu.VMEM((8, 2, 2, few, features), bf16),
            pltpu.VMEM((8, 2, few, features), bf16),
            pltpu.VMEM((8, 2, few, features), bf16),
            pltpu.VMEM((2, 3, 2, few, features), bf16),
            pltpu.VMEM((2, 2, few, features), bf16),
            pltpu.VMEM((3, few, features), bf16),
            dma((4,)), dma((28,)), dma((8, 4)), dma((8, 2)), dma((8, 2)), dma((8, 2)), dma((2, 3, 2)),
            dma((2, 2)), dma((3,)), dma((3,)), dma((3,)), dma((3,)), dma((3,)), dma((4,)), dma((4,)),
        ],
        compiler_params=pltpu.CompilerParams(
            collective_id=0, has_side_effects=True, vmem_limit_bytes=48 * 1024 * 1024
        ),
        name="exchange",
    )(*held, round_seed)
    total, input_rows = (pltpu.with_memory_space_constraint(v, pltpu.VMEM) for v in (total, input_rows))
    return pl.pallas_call(
        store_kernel,
        out_shape=(jax.ShapeDtypeStruct((features, ff), f32), jax.ShapeDtypeStruct((few, features), bf16)),
        in_specs=[vmem, vmem],
        out_specs=(hbm, hbm),
        scratch_shapes=[dma((9,))],
        compiler_params=pltpu.CompilerParams(vmem_limit_bytes=4 * 1024 * 1024),
        name="store",
    )(total, input_rows)


def solution(mesh):
    placed = (P("col", "row"), P("row", "col"), P("row", "col"), P(), P("row"))
    return jax.shard_map(
        shards,
        mesh=mesh,
        in_specs=placed,
        out_specs=(P("row", "col"), P("col", "row")),
        check_vma=False,
    )
```

time: 249 us -> 61 us (0.24)
  waiting for transfers between devices: 207 us -> 0 us
  Pallas kernels: 0 us -> 59.6 us
  matrix products: 16.3 us -> 0 us
  between operations: 14.6 us -> 1.28 us
  local copies, waits for them, and re-layouts: 7.62 us -> 0 us
  other arithmetic: 2.49 us -> 0 us
    all_gather x2 -> x0, waiting for transfers between devices: 129 us -> none  [the longest x1 79 us: shards(): everything = lax.all_gather(quantized, 'row', axis=0, tiled=True)]
    reduce_scatter x1 -> x0, waiting for transfers between devices: 77.1 us -> none  [shards(): lax.psum_scatter(project(everything, up_weight).astype(jnp.bfloat16), 'co...]
    pallas_call x0 -> x2, Pallas kernels: none -> 59.6 us  [the longest x1 56.7 us: shards(): pl.pallas_call(exchange_kernel, out_shape=(pltpu.VMEM((features, ff), f32...]
    dot_general x2 -> x0, matrix products: 16.3 us -> none  [the longest x1 9.16 us: contract(): lax.dot_general(left, right, (((0,), (0,)), ((), ())), preferred_element_...]
    unnamed x3 -> x0, local copies, waits for them, and re-layouts: 7.62 us -> none
  transfers between devices with their start and end apart: 3 -> 0, of which waited for: 3 -> 0; matrix products, arithmetic and copies ran while one was open for 10% -> 0% of each run, Pallas kernels for 0% -> 0%
where the time goes in v2:
time: 61 us; the launch traced here: 60.9 us
  Pallas kernels  59.6 us (98%)
  between operations  1.28 us (2%)
    pallas_call x1, Pallas kernels, shards(): pl.pallas_call(exchange_kernel, out_shape=(pltpu.VMEM((features, ff), f32...  56.7 us
    pallas_call x1, Pallas kernels, shards(): pl.pallas_call(store_kernel, out_shape=(jax.ShapeDtypeStruct((features, f...  2.92 us

profile of v2, /device:TPU:36, one launch (start us, length us, event | category | flops | bytes accessed | tf_op | source)
XLA Modules:
  0.0 60.9 jit_solution(6613024667314806692)
XLA Ops:
  1.3 56.7 %exchange.1 = (f32[1024,1664]{1,0:T(8,128)S(1)}, bf16[32,1024]{1,0:T(8,128)(2,1)S(1)}) custom-call(bf16[32,1024]{1,0:T(8,128)(2,1)} %act_hbm.1, bf16[1024,1664]{1,0:T(8,128)(2,1)} %weight_hbm.1, bf16[128,1664]{1,0:T(8,128)(2,1)} %grad_hbm.1, s32[1,128]{1,0:T(1,128)} %bitcast.1, s32[1]{0:T(128)S(6)} %copy.7.seed_ref), custom_call_target="tpu_custom_call" | custom-call | tf_op jit(solution)/shard_map/exchange/pallas_call | solution.py:336
  58.0 2.9 %store.1 = (f32[1024,1664]{1,0:T(8,128)}, bf16[32,1024]{1,0:T(8,128)(2,1)}) custom-call(f32[1024,1664]{1,0:T(8,128)S(1)} %get-tuple-element.4.total_ref, bf16[32,1024]{1,0:T(8,128)(2,1)S(1)} %get-tuple-element.5.rows_ref), custom_call_target="tpu_custom_call" | custom-call | tf_op jit(solution)/shard_map/store/pallas_call | solution.py:364

commit v3 on v2

--- a/solution.py
+++ b/solution.py
@@ -9,7 +9,6 @@
 NX, NY, NH = 4, 4, 4
 OWN, LEFT, RIGHT, FAR, OWN2, LEFT2, RIGHT2, FAR2 = range(8)
 SHARDS = ((0, 0), (3, 0), (1, 0), (2, 0), (0, 1), (3, 1), (1, 1), (2, 1))
-WIDE = 512
 
 
 def device(x, lo, y, hi, core):
@@ -45,8 +44,6 @@
     def root(i):
         return lax.rem(x + SHARDS[i][0], NX)
 
-    def slot(i):
-        return root(i) * 2 + lo_of(i)
 
     def remote(src, dst, send, recv, to):
         return pltpu.make_async_remote_copy(
@@ -75,34 +72,39 @@
     mixed_seed = seed_ref[0] * jnp.int32(1013904223)
     first = col * ff
 
-    def round_columns(n, _):
-        columns = pl.ds(pl.multiple_of(n * 128, 128), 128)
-        counter = base + (first + n * 128 + lax.broadcasted_iota(jnp.int32, (tokens, 128), 1))
-        mixed = counter * jnp.int32(747796405) + mixed_seed
-        mixed = mixed ^ (mixed >> 15)
-        mixed = mixed * jnp.int32(277803737)
-        mixed = mixed ^ (mixed >> 16)
-        level = (mixed & 255).astype(jnp.float32)
-        scaled = grad[:, columns].astype(jnp.float32) * 4.0 + (level + 0.5) / 256.0
-        rounded = (jnp.floor(scaled) / 4.0).astype(jnp.bfloat16)
-        g_ref[slot(OWN), :, :, columns] = rounded.reshape(4, block, 128)
-        return 0
-
-    lax.fori_loop(0, ff // 128, round_columns, 0)
+    def round_rows(half):
+        rows = slice(half * 2 * block, (half + 1) * 2 * block)
+
+        def round_columns(n, _):
+            columns = pl.ds(pl.multiple_of(n * 128, 128), 128)
+            counter = base[rows] + (first + n * 128 + lax.broadcasted_iota(jnp.int32, (2 * block, 128), 1))
+            mixed = counter * jnp.int32(747796405) + mixed_seed
+            mixed = mixed ^ (mixed >> 15)
+            mixed = mixed * jnp.int32(277803737)
+            mixed = mixed ^ (mixed >> 16)
+            level = (mixed & 255).astype(jnp.float32)
+            scaled = grad[rows, columns].astype(jnp.float32) * 4.0 + (level + 0.5) / 256.0
+            rounded = (jnp.floor(scaled) / 4.0).astype(jnp.bfloat16)
+            g_ref[x, lo, pl.ds(2 * half, 2), :, columns] = rounded.reshape(2, block, 128)
+            return 0
+
+        lax.fori_loop(0, ff // 128, round_columns, 0)
+
+    round_rows(0)
     pl.semaphore_wait(barrier, len(peers))
 
     sends = []
 
     def send_g(i, j, to):
-        where = g_ref.at[slot(i), j]
-        copy = remote(where, where, gs.at[len(sends)], gr.at[slot(i), j], to)
+        where = g_ref.at[root(i), lo_of(i), j]
+        copy = remote(where, where, gs.at[len(sends)], gr.at[root(i), lo_of(i), j], to)
         copy.start()
         sends.append(copy)
 
     def wait_g(i, *js):
         for j in js:
-            where = g_ref.at[slot(i), j]
-            remote(where, where, gs.at[0], gr.at[slot(i), j], here).wait_recv()
+            where = g_ref.at[root(i), lo_of(i), j]
+            remote(where, where, gs.at[0], gr.at[root(i), lo_of(i), j], here).wait_recv()
 
     def core_copy(i, q):
         return remote(part.at[i, q, 1 - core], crecv.at[i, q], cs.at[i, q], cr.at[i, q], sibling)
@@ -110,19 +112,14 @@
     def project(*units):
         rows = 2 * block
 
-        def step(n, _):
-            wide = pl.ds(pl.multiple_of(n * WIDE, WIDE), WIDE)
-            left_side = jnp.concatenate(
-                [g_ref[slot(i), pl.ds(2 * q, 2)].reshape(rows, ff) for i, q in units], axis=0
-            )
-            value = lax.dot_general(
-                left_side, turned[:, wide], (((1,), (0,)), ((), ())), preferred_element_type=jnp.float32
-            ).astype(jnp.bfloat16)
-            for u, (i, q) in enumerate(units):
-                part[i, q, :, :, wide] = value[u * rows : (u + 1) * rows].reshape(2, block, WIDE)
-            return 0
-
-        lax.fori_loop(0, features // WIDE, step, 0)
+        left_side = jnp.concatenate(
+            [g_ref[root(i), lo_of(i), pl.ds(2 * q, 2)].reshape(rows, ff) for i, q in units], axis=0
+        )
+        value = lax.dot_general(
+            left_side, turned[...], (((1,), (0,)), ((), ())), preferred_element_type=jnp.float32
+        ).astype(jnp.bfloat16)
+        for u, (i, q) in enumerate(units):
+            part[i, q] = value[u * rows : (u + 1) * rows].reshape(2, block, features)
         for i, q in units:
             core_copy(i, q).start()
 
@@ -169,13 +166,15 @@
         where = a_ref.at[y, lax.rem(hi + NH - d, NH), core]
         remote(where, where, azs.at[d - 1], azr.at[d - 1], here).wait_recv()
 
-    def ay_copy(d):
-        where = a_ref.at[y, :, core]
-        return remote(where, where, ays.at[d - 1], ayr.at[d - 1], at_y(lax.rem(y + d, NY)))
-
-    def ay_wait(d):
-        where = a_ref.at[lax.rem(y + NY - d, NY), :, core]
-        remote(where, where, ays.at[d - 1], ayr.at[d - 1], here).wait_recv()
+    def ay_copy(n):
+        up, down = lax.rem(y + 1, NY), lax.rem(y + NY - 1, NY)
+        owner, half, to, k = ((y, 0, up, 0), (y, 1, down, 2), (y, 1, up, 0), (y, 0, down, 2), (down, 0, up, 1), (up, 1, down, 1))[n]
+        where = a_ref.at[owner, pl.ds(2 * half, 2), core]
+        return remote(where, where, ays.at[n], ayr.at[k, half], at_y(to))
+
+    def ay_wait(d, half):
+        where = a_ref.at[lax.rem(y + NY - d, NY), pl.ds(2 * half, 2), core]
+        remote(where, where, ays.at[0], ayr.at[d - 1, half], here).wait_recv()
 
     def ac_copy(d):
         where = a_ref.at[lax.rem(y + NY - d, NY), :, core]
@@ -190,28 +189,32 @@
             rows = a_ref[r, pl.ds(2 * plane, 2)].reshape(tokens, features)
             turned_act[:, r * tokens : (r + 1) * tokens] = jnp.transpose(rows)
 
-    def accumulate(plane, lowest, highest, last):
-        for r in range(0, features, 256):
-            value = jnp.zeros((256, highest - lowest), jnp.float32)
-            for k in range(NX):
-                value += lax.dot_general(
-                    turned_act[r : r + 256, k * tokens : (k + 1) * tokens],
-                    g_ref[2 * k + plane, :, :, lowest:highest].reshape(tokens, highest - lowest),
-                    (((1,), (0,)), ((), ())),
-                    preferred_element_type=jnp.float32,
-                )
-            if last:
-                value = (total_ref[r : r + 256, lowest:highest] + value) * (NX * 2 * tokens) ** (-0.5)
-            total_ref[r : r + 256, lowest:highest] = value
+    def accumulate(plane, span, last):
+        lowest, highest = span
+        value = lax.dot_general(
+            turned_act[...],
+            g_ref[:, plane, :, :, lowest:highest].reshape(NX * tokens, highest - lowest),
+            (((1,), (0,)), ((), ())),
+            preferred_element_type=jnp.float32,
+        )
+        if last:
+            value = (total_ref[:, lowest:highest] + value) * (NX * 2 * tokens) ** (-0.5)
+        total_ref[:, lowest:highest] = value
 
     spans = [(n, min(n + 512, ff)) for n in range(0, ff, 512)]
 
     for d in (1, 2, 3):
         az_copy(d).start()
-    for j, k, p in ((0, 3, 0), (1, 2, 3), (2, 1, 1), (3, 0, 2)):
+    send_g(OWN, 0, right)
+    send_g(OWN, 1, left)
+    send_g(OWN, 0, pair)
+    send_g(OWN, 1, pair)
+    round_rows(1)
+    for j, k in ((2, 3), (1, 0), (3, 2)):
         send_g(OWN, j, right)
         send_g(OWN, k, left)
-        send_g(OWN, p, pair)
+    send_g(OWN, 2, pair)
+    send_g(OWN, 3, pair)
     loads[3].wait()
 
     def turn_weight(n, _):
@@ -223,68 +226,80 @@
     project((OWN, 0), (OWN, 1))
     wait_g(LEFT, 0)
     send_g(LEFT, 0, right)
+    wait_g(RIGHT, 1)
+    send_g(RIGHT, 1, left)
+    add_cores((OWN, 0), (OWN, 1))
+    wait_g(LEFT, 2)
+    send_g(LEFT, 2, right)
     wait_g(RIGHT, 3)
     send_g(RIGHT, 3, left)
-    add_cores((OWN, 0), (OWN, 1))
-    wait_g(LEFT, 1)
-    send_g(LEFT, 1, right)
-    wait_g(RIGHT, 2)
-    send_g(RIGHT, 2, left)
     for d in (1, 2, 3):
         az_wait(d)
-    for d in (1, 2, 3):
-        ay_copy(d).start()
+    for n in range(4):
+        ay_copy(n).start()
     ac_copy(0).start()
     wait_g(OWN2, 0)
     send_g(OWN2, 0, right)
-    wait_g(OWN2, 3)
-    send_g(OWN2, 3, left)
-    wait_g(LEFT, 2, 3)
-    wait_g(RIGHT, 1, 0)
+    send_g(OWN2, 0, left)
+    wait_g(LEFT, 1, 3)
+    wait_g(RIGHT, 0, 2)
     project((LEFT, 0), (LEFT, 1), (RIGHT, 0), (RIGHT, 1))
     wait_g(OWN2, 1)
     send_g(OWN2, 1, right)
+    send_g(OWN2, 1, left)
+    wait_g(FAR, 0, 1)
+    send_g(FAR, 0, pair)
+    send_g(FAR, 1, pair)
+    ay_wait(1, 0)
+    ay_copy(4).start()
+    ay_wait(3, 1)
+    ay_copy(5).start()
     wait_g(OWN2, 2)
+    send_g(OWN2, 2, right)
     send_g(OWN2, 2, left)
-    for j, k in ((2, 1), (3, 0)):
-        send_g(OWN2, j, right)
-        send_g(OWN2, k, left)
     add_cores((LEFT, 0), (LEFT, 1), (RIGHT, 0), (RIGHT, 1))
-    wait_g(FAR, 0, 3)
-    send_g(FAR, 0, pair)
+    wait_g(FAR, 2, 3)
+    send_g(FAR, 2, pair)
     send_g(FAR, 3, pair)
+    wait_g(OWN2, 3)
+    send_g(OWN2, 3, right)
+    send_g(OWN2, 3, left)
+    project((OWN2, 0), (OWN2, 1), (FAR, 0), (FAR, 1))
     add_columns((OWN, 0), (OWN, 1))
-    wait_g(FAR, 1, 2)
-    send_g(FAR, 1, pair)
-    send_g(FAR, 2, pair)
-    project((OWN2, 0), (OWN2, 1), (FAR, 0), (FAR, 1))
     add_cores((OWN2, 0), (OWN2, 1), (FAR, 0), (FAR, 1))
-    for d in (1, 2, 3):
-        ay_wait(d)
-        ac_copy(d).start()
-    add_columns((LEFT, 0), (LEFT, 1), (RIGHT, 0), (RIGHT, 1))
     wait_g(LEFT2, 0, 1)
-    wait_g(RIGHT2, 3, 2)
-    project((LEFT2, 0), (RIGHT2, 1))
+    wait_g(RIGHT2, 0, 1)
+    wait_g(FAR2, 0, 1)
+    project((LEFT2, 0), (RIGHT2, 0), (FAR2, 0))
+    ay_wait(1, 1)
+    ac_copy(1).start()
+    ay_wait(3, 0)
+    ac_copy(3).start()
+    ay_wait(2, 0)
+    ay_wait(2, 1)
+    ac_copy(2).start()
+    add_cores((LEFT2, 0), (RIGHT2, 0), (FAR2, 0))
     for d in range(4):
         ac_wait(d)
-    add_cores((LEFT2, 0), (RIGHT2, 1))
     turn_act(lo)
-    for span in spans:
-        accumulate(lo, *span, False)
+    for span in spans[:2]:
+        accumulate(lo, span, False)
+    wait_g(LEFT2, 2, 3)
+    wait_g(RIGHT2, 2, 3)
+    wait_g(FAR2, 2, 3)
+    project((LEFT2, 1), (RIGHT2, 1), (FAR2, 1))
+    add_columns((LEFT, 0), (LEFT, 1), (RIGHT, 0), (RIGHT, 1))
+    add_cores((LEFT2, 1), (RIGHT2, 1), (FAR2, 1))
     add_columns((OWN2, 0), (OWN2, 1), (FAR, 0), (FAR, 1))
+    for span in spans[2:]:
+        accumulate(lo, span, False)
     turn_act(1 - lo)
-    wait_g(LEFT2, 2, 3)
-    wait_g(RIGHT2, 1, 0)
-    wait_g(FAR2, 0, 3, 1, 2)
-    project((LEFT2, 1), (RIGHT2, 0), (FAR2, 0), (FAR2, 1))
-    accumulate(1 - lo, *spans[0], True)
-    add_cores((LEFT2, 1), (RIGHT2, 0), (FAR2, 0), (FAR2, 1))
-    for span in spans[1:3]:
-        accumulate(1 - lo, *span, True)
-    add_columns((LEFT2, 0), (RIGHT2, 1), (LEFT2, 1), (RIGHT2, 0), (FAR2, 0), (FAR2, 1))
+    add_columns((LEFT2, 0), (RIGHT2, 0), (FAR2, 0))
+    for span in spans[:3]:
+        accumulate(1 - lo, span, True)
+    add_columns((LEFT2, 1), (RIGHT2, 1), (FAR2, 1))
     for span in spans[3:]:
-        accumulate(1 - lo, *span, True)
+        accumulate(1 - lo, span, True)
 
     total = tsum[lax.div(hi, 2), lax.rem(hi, 2)].astype(jnp.float32)
     for k in range(3):
@@ -308,7 +323,8 @@
 
     for d in (1, 2, 3):
         az_copy(d).wait_send()
-        ay_copy(d).wait_send()
+    for n in range(6):
+        ay_copy(n).wait_send()
     for d in range(4):
         ac_copy(d).wait_send()
 
@@ -339,7 +355,7 @@
         in_specs=[hbm] * 4 + [pl.BlockSpec(memory_space=pltpu.SMEM)],
         out_specs=(vmem, vmem),
         scratch_shapes=[
-            pltpu.VMEM((8, 4, tokens // 4, ff), bf16),
+            pltpu.VMEM((NX, 2, 4, tokens // 4, ff), bf16),
             pltpu.VMEM((NY, NH, 2, few, features), bf16),
             pltpu.VMEM((tokens, ff), bf16),
             pltpu.VMEM((features, ff), bf16),
@@ -352,8 +368,8 @@
             pltpu.VMEM((2, 3, 2, few, features), bf16),
             pltpu.VMEM((2, 2, few, features), bf16),
             pltpu.VMEM((3, few, features), bf16),
-            dma((4,)), dma((28,)), dma((8, 4)), dma((8, 2)), dma((8, 2)), dma((8, 2)), dma((2, 3, 2)),
-            dma((2, 2)), dma((3,)), dma((3,)), dma((3,)), dma((3,)), dma((3,)), dma((4,)), dma((4,)),
+            dma((4,)), dma((28,)), dma((NX, 2, 4)), dma((8, 2)), dma((8, 2)), dma((8, 2)), dma((2, 3, 2)),
+            dma((2, 2)), dma((3,)), dma((3,)), dma((3,)), dma((6,)), dma((3, 2)), dma((4,)), dma((4,)),
         ],
         compiler_params=pltpu.CompilerParams(
             collective_id=0, has_side_effects=True, vmem_limit_bytes=48 * 1024 * 1024

time: 61 us -> 53.1 us (0.87)
  the two profiles are of different devices: /device:TPU:36 before, /device:TPU:112 now
where the time goes in v3:
time: 53.1 us; the launch traced here: 53 us
  Pallas kernels  51.8 us (98%)
  between operations  1.28 us (2%)
    pallas_call x1, Pallas kernels, shards(): pl.pallas_call(exchange_kernel, out_shape=(pltpu.VMEM((features, ff), f32...  48.8 us
    pallas_call x1, Pallas kernels, shards(): pl.pallas_call(store_kernel, out_shape=(jax.ShapeDtypeStruct((features, f...  2.92 us

profile of v3, /device:TPU:112, one launch (start us, length us, event | category | flops | bytes accessed | tf_op | source)
XLA Modules:
  0.0 53.0 jit_solution(10407992368325951970)
XLA Ops:
  1.3 48.8 %exchange.1 = (f32[1024,1664]{1,0:T(8,128)S(1)}, bf16[32,1024]{1,0:T(8,128)(2,1)S(1)}) custom-call(bf16[32,1024]{1,0:T(8,128)(2,1)} %act_hbm.1, bf16[1024,1664]{1,0:T(8,128)(2,1)} %weight_hbm.1, bf16[128,1664]{1,0:T(8,128)(2,1)} %grad_hbm.1, s32[1,128]{1,0:T(1,128)} %bitcast.1, s32[1]{0:T(128)S(6)} %copy.7.seed_ref), custom_call_target="tpu_custom_call" | custom-call | tf_op jit(solution)/shard_map/exchange/pallas_call | solution.py:352
  50.1 2.9 %store.1 = (f32[1024,1664]{1,0:T(8,128)}, bf16[32,1024]{1,0:T(8,128)(2,1)}) custom-call(f32[1024,1664]{1,0:T(8,128)S(1)} %get-tuple-element.4.total_ref, bf16[32,1024]{1,0:T(8,128)(2,1)S(1)} %get-tuple-element.5.rows_ref), custom_call_target="tpu_custom_call" | custom-call | tf_op jit(solution)/shard_map/store/pallas_call | solution.py:380

commit v4 on v3

--- a/solution.py
+++ b/solution.py
@@ -17,8 +17,8 @@
 
 def exchange_kernel(
     act_hbm, weight_hbm, grad_hbm, base_hbm, seed_ref, total_ref, out_ref,
-    g_ref, a_ref, grad, weight, turned, turned_act, base_row, part, crecv, ssum, yrecv, tsum, zrecv,
-    lsem, gs, gr, cs, cr, ys, yr, zs, zr, azs, azr, ays, ayr, acs, acr,
+    g_ref, a_ref, grad, weight, turned, turned_act, base_row, part, crecv, ssum, yrecv, tsum, zrecv, zpair, zfar,
+    lsem, gs, gr, hr, cs, cr, ys, yr, zs, zr, ts, tr, azs, azr, ays, ayr, acs, acr,
 ):
     row, col = lax.axis_index("row"), lax.axis_index("col")
     x, lo = lax.div(row, 2), lax.rem(row, 2)
@@ -56,7 +56,7 @@
         pltpu.make_async_copy(act_hbm, a_ref.at[y, hi, core], lsem.at[2]),
         pltpu.make_async_copy(weight_hbm, weight, lsem.at[3]),
     ]
-    for load in loads:
+    for load in loads[:3]:
         load.start()
 
     barrier = pltpu.get_barrier_semaphore()
@@ -68,16 +68,17 @@
 
     for load in loads[:3]:
         load.wait()
+    loads[3].start()
     base = jnp.transpose(jnp.broadcast_to(base_row[...], (tokens, tokens)))
     mixed_seed = seed_ref[0] * jnp.int32(1013904223)
     first = col * ff
 
-    def round_rows(half):
-        rows = slice(half * 2 * block, (half + 1) * 2 * block)
+    def round_rows(j, count):
+        rows = slice(j * block, (j + count) * block)
 
         def round_columns(n, _):
             columns = pl.ds(pl.multiple_of(n * 128, 128), 128)
-            counter = base[rows] + (first + n * 128 + lax.broadcasted_iota(jnp.int32, (2 * block, 128), 1))
+            counter = base[rows] + (first + n * 128 + lax.broadcasted_iota(jnp.int32, (count * block, 128), 1))
             mixed = counter * jnp.int32(747796405) + mixed_seed
             mixed = mixed ^ (mixed >> 15)
             mixed = mixed * jnp.int32(277803737)
@@ -85,12 +86,12 @@
             level = (mixed & 255).astype(jnp.float32)
             scaled = grad[rows, columns].astype(jnp.float32) * 4.0 + (level + 0.5) / 256.0
             rounded = (jnp.floor(scaled) / 4.0).astype(jnp.bfloat16)
-            g_ref[x, lo, pl.ds(2 * half, 2), :, columns] = rounded.reshape(2, block, 128)
+            g_ref[x, lo, pl.ds(j, count), :, columns] = rounded.reshape(count, block, 128)
             return 0
 
         lax.fori_loop(0, ff // 128, round_columns, 0)
 
-    round_rows(0)
+    round_rows(0, 1)
     pl.semaphore_wait(barrier, len(peers))
 
     sends = []
@@ -106,20 +107,35 @@
             where = g_ref.at[root(i), lo_of(i), j]
             remote(where, where, gs.at[0], gr.at[root(i), lo_of(i), j], here).wait_recv()
 
+    def half_chunk(i, half):
+        return g_ref.at[root(i), lo_of(i), 3, pl.ds(half * (block // 2), block // 2)]
+
+    def send_half(i, half, to):
+        copy = remote(half_chunk(i, half), half_chunk(i, half), gs.at[len(sends)], hr.at[half], to)
+        copy.start()
+        sends.append(copy)
+
+    def wait_half(half):
+        where = half_chunk(FAR2, half)
+        remote(where, where, gs.at[0], hr.at[half], here).wait_recv()
+
     def core_copy(i, q):
         return remote(part.at[i, q, 1 - core], crecv.at[i, q], cs.at[i, q], cr.at[i, q], sibling)
 
-    def project(*units):
-        rows = 2 * block
-
+    def project(*pieces):
         left_side = jnp.concatenate(
-            [g_ref[root(i), lo_of(i), pl.ds(2 * q, 2)].reshape(rows, ff) for i, q in units], axis=0
+            [g_ref[root(i), lo_of(i), pl.ds(j, n)].reshape(n * block, ff) for i, j, n in pieces], axis=0
         )
         value = lax.dot_general(
             left_side, turned[...], (((1,), (0,)), ((), ())), preferred_element_type=jnp.float32
         ).astype(jnp.bfloat16)
-        for u, (i, q) in enumerate(units):
-            part[i, q] = value[u * rows : (u + 1) * rows].reshape(2, block, features)
+        row = 0
+        for i, j, n in pieces:
+            for k in range(j, j + n):
+                part[i, k // 2, k % 2] = value[row : row + block]
+                row += block
+
+    def send_core(*units):
         for i, q in units:
             core_copy(i, q).start()
 
@@ -136,27 +152,57 @@
             def _():
                 y_copy(i, q).start()
 
-    def z_copy(lo_root, q):
-        to = 2 * lo_root + q
+    def z_copy(q):
+        to = 2 * (1 - lo) + q
         k = lax.rem(hi + NH - to, NH) - 1
-        return remote(tsum.at[lo_root, q], zrecv.at[k], zs.at[lo_root, q], zr.at[k], at_hi(to))
+        return remote(tsum.at[1 - lo, q], zrecv.at[k], zs.at[q], zr.at[k], at_hi(to))
+
+    def sum_columns(i, q):
+        lo_root = lo_of(i)
+        total = ssum[i, q].astype(jnp.float32)
+        for k in range(3):
+            where = yrecv.at[lo_root, k, q]
+            remote(where, where, ys.at[i, q], yr.at[lo_root, k, q], here).wait_recv()
+            total += yrecv[lo_root, k, q].astype(jnp.float32)
+        tsum[lo_root, q] = total.astype(jnp.bfloat16)
 
     def add_columns(*units):
         for i, q in units:
 
             @pl.when(y == root(i))
             def _():
-                lo_root = lo_of(i)
-                total = ssum[i, q].astype(jnp.float32)
-                for k in range(3):
-                    where = yrecv.at[lo_root, k, q]
-                    remote(where, where, ys.at[i, q], yr.at[lo_root, k, q], here).wait_recv()
-                    total += yrecv[lo_root, k, q].astype(jnp.float32)
-                tsum[lo_root, q] = total.astype(jnp.bfloat16)
-
-                @pl.when(hi != 2 * lo_root + q)
+                sum_columns(i, q)
+
+                @pl.when(hi != 2 * (1 - lo) + q)
                 def _():
-                    z_copy(lo_root, q).start()
+                    z_copy(q).start()
+
+    parity = lax.rem(hi, 2)
+    far = lax.rem(lax.div(hi, 2) + lo, 2)
+    keep = lax.rem(parity + far, 2)
+
+    def pair_copy():
+        return remote(tsum.at[lo, 1 - keep], zpair, ts.at[0], tr.at[0], at_hi(hi + 1 - 2 * parity))
+
+    def far_copy():
+        return remote(tsum.at[lo, keep], zfar, ts.at[1], tr.at[1], at_hi(lax.rem(hi + 3 - 2 * parity, NH)))
+
+    def add_plane(*shards):
+        for i in shards:
+
+            @pl.when(y == root(i))
+            def _():
+                for q in range(2):
+                    sum_columns(i, q)
+                pair_copy().start()
+
+    def pass_on():
+        remote(zpair, zpair, ts.at[0], tr.at[0], here).wait_recv()
+
+        @pl.when(far == 1)
+        def _():
+            tsum[lo, keep] = (tsum[lo, keep].astype(jnp.float32) + zpair[...].astype(jnp.float32)).astype(jnp.bfloat16)
+            far_copy().start()
 
     def az_copy(d):
         where = a_ref.at[y, hi, core]
@@ -206,15 +252,16 @@
     for d in (1, 2, 3):
         az_copy(d).start()
     send_g(OWN, 0, right)
+    round_rows(1, 1)
     send_g(OWN, 1, left)
+    round_rows(2, 2)
+    send_g(OWN, 3, pair)
     send_g(OWN, 0, pair)
-    send_g(OWN, 1, pair)
-    round_rows(1)
     for j, k in ((2, 3), (1, 0), (3, 2)):
         send_g(OWN, j, right)
         send_g(OWN, k, left)
+    send_g(OWN, 1, pair)
     send_g(OWN, 2, pair)
-    send_g(OWN, 3, pair)
     loads[3].wait()
 
     def turn_weight(n, _):
@@ -223,7 +270,8 @@
         return 0
 
     lax.fori_loop(0, features // 128, turn_weight, 0)
-    project((OWN, 0), (OWN, 1))
+    project((OWN, 0, 4))
+    send_core((OWN, 0), (OWN, 1))
     wait_g(LEFT, 0)
     send_g(LEFT, 0, right)
     wait_g(RIGHT, 1)
@@ -238,15 +286,16 @@
     for n in range(4):
         ay_copy(n).start()
     ac_copy(0).start()
+    wait_g(OWN2, 3)
+    send_g(OWN2, 3, right)
+    send_g(OWN2, 3, left)
+    wait_g(LEFT, 1, 3)
+    wait_g(RIGHT, 0, 2)
+    project((LEFT, 0, 4), (RIGHT, 0, 4))
+    send_core((LEFT, 0), (LEFT, 1), (RIGHT, 0), (RIGHT, 1))
     wait_g(OWN2, 0)
     send_g(OWN2, 0, right)
     send_g(OWN2, 0, left)
-    wait_g(LEFT, 1, 3)
-    wait_g(RIGHT, 0, 2)
-    project((LEFT, 0), (LEFT, 1), (RIGHT, 0), (RIGHT, 1))
-    wait_g(OWN2, 1)
-    send_g(OWN2, 1, right)
-    send_g(OWN2, 1, left)
     wait_g(FAR, 0, 1)
     send_g(FAR, 0, pair)
     send_g(FAR, 1, pair)
@@ -254,58 +303,121 @@
     ay_copy(4).start()
     ay_wait(3, 1)
     ay_copy(5).start()
-    wait_g(OWN2, 2)
-    send_g(OWN2, 2, right)
-    send_g(OWN2, 2, left)
+    wait_g(OWN2, 1)
+    send_g(OWN2, 1, right)
+    send_g(OWN2, 1, left)
     add_cores((LEFT, 0), (LEFT, 1), (RIGHT, 0), (RIGHT, 1))
     wait_g(FAR, 2, 3)
     send_g(FAR, 2, pair)
-    send_g(FAR, 3, pair)
-    wait_g(OWN2, 3)
-    send_g(OWN2, 3, right)
-    send_g(OWN2, 3, left)
-    project((OWN2, 0), (OWN2, 1), (FAR, 0), (FAR, 1))
-    add_columns((OWN, 0), (OWN, 1))
-    add_cores((OWN2, 0), (OWN2, 1), (FAR, 0), (FAR, 1))
-    wait_g(LEFT2, 0, 1)
-    wait_g(RIGHT2, 0, 1)
-    wait_g(FAR2, 0, 1)
-    project((LEFT2, 0), (RIGHT2, 0), (FAR2, 0))
+    wait_g(OWN2, 2)
+    project((FAR, 0, 4), (OWN2, 0, 4))
+    send_core((FAR, 0), (FAR, 1), (OWN2, 0), (OWN2, 1))
+    wait_g(LEFT2, 3)
+    send_half(LEFT2, 0, right)
+    send_g(OWN2, 2, right)
+    wait_g(RIGHT2, 3)
+    send_half(RIGHT2, 1, left)
+    send_g(OWN2, 2, left)
+    add_plane(OWN)
     ay_wait(1, 1)
     ac_copy(1).start()
     ay_wait(3, 0)
     ac_copy(3).start()
+    add_cores((FAR, 0), (FAR, 1), (OWN2, 0), (OWN2, 1))
+    wait_g(LEFT2, 0)
+    wait_g(RIGHT2, 0)
+    wait_g(FAR2, 0)
+    project((LEFT2, 3, 1), (RIGHT2, 3, 1), (LEFT2, 0, 1), (RIGHT2, 0, 1), (FAR2, 0, 1))
+
+    @pl.when(core == 0)
+    def _():
+        send_core((LEFT2, 1), (RIGHT2, 1))
+
+    @pl.when(core == 1)
+    def _():
+        send_core((FAR2, 0), (LEFT2, 0), (RIGHT2, 0))
+
     ay_wait(2, 0)
     ay_wait(2, 1)
     ac_copy(2).start()
-    add_cores((LEFT2, 0), (RIGHT2, 0), (FAR2, 0))
+    wait_g(LEFT2, 1)
+    wait_g(RIGHT2, 1)
+    wait_g(FAR2, 1)
+    project((LEFT2, 1, 1), (RIGHT2, 1, 1), (FAR2, 1, 1))
+
+    @pl.when(core == 0)
+    def _():
+        send_core((FAR2, 0), (LEFT2, 0), (RIGHT2, 0))
+        add_cores((FAR2, 0), (LEFT2, 0), (RIGHT2, 0))
+
+    @pl.when(core == 1)
+    def _():
+        add_cores((LEFT2, 1), (RIGHT2, 1))
+
+    wait_half(0)
+    wait_half(1)
+    project((FAR2, 3, 1))
+
+    @pl.when(core == 0)
+    def _():
+        send_core((FAR2, 1))
+
+    wait_g(LEFT2, 2)
+    wait_g(RIGHT2, 2)
+    wait_g(FAR2, 2)
+    project((LEFT2, 2, 1), (RIGHT2, 2, 1), (FAR2, 2, 1))
+
+    @pl.when(core == 1)
+    def _():
+        send_core((FAR2, 1), (LEFT2, 1), (RIGHT2, 1))
+        add_cores((FAR2, 0), (LEFT2, 0), (RIGHT2, 0), (FAR2, 1))
+
+    add_plane(FAR, LEFT, RIGHT)
+    add_columns((OWN2, 0), (OWN2, 1))
     for d in range(4):
         ac_wait(d)
     turn_act(lo)
-    for span in spans[:2]:
-        accumulate(lo, span, False)
-    wait_g(LEFT2, 2, 3)
-    wait_g(RIGHT2, 2, 3)
-    wait_g(FAR2, 2, 3)
-    project((LEFT2, 1), (RIGHT2, 1), (FAR2, 1))
-    add_columns((LEFT, 0), (LEFT, 1), (RIGHT, 0), (RIGHT, 1))
-    add_cores((LEFT2, 1), (RIGHT2, 1), (FAR2, 1))
-    add_columns((OWN2, 0), (OWN2, 1), (FAR, 0), (FAR, 1))
+
+    @pl.when(core == 0)
+    def _():
+        add_cores((FAR2, 1), (LEFT2, 1), (RIGHT2, 1))
+
+    @pl.when(core == 1)
+    def _():
+        add_columns((LEFT2, 1), (RIGHT2, 1))
+
+    accumulate(lo, spans[0], False)
+    accumulate(lo, spans[1], False)
+    add_columns((FAR2, 0), (LEFT2, 0), (RIGHT2, 0))
+    pass_on()
     for span in spans[2:]:
         accumulate(lo, span, False)
     turn_act(1 - lo)
-    add_columns((LEFT2, 0), (RIGHT2, 0), (FAR2, 0))
-    for span in spans[:3]:
+
+    @pl.when(core == 0)
+    def _():
+        add_columns((FAR2, 1), (LEFT2, 1), (RIGHT2, 1))
+
+    @pl.when(core == 1)
+    def _():
+        add_columns((FAR2, 1))
+
+    for span in spans:
         accumulate(1 - lo, span, True)
-    add_columns((LEFT2, 1), (RIGHT2, 1), (FAR2, 1))
-    for span in spans[3:]:
-        accumulate(1 - lo, span, True)
-
-    total = tsum[lax.div(hi, 2), lax.rem(hi, 2)].astype(jnp.float32)
-    for k in range(3):
-        remote(zrecv.at[k], zrecv.at[k], zs.at[0, 0], zr.at[k], here).wait_recv()
-        total += zrecv[k].astype(jnp.float32)
-    out_ref[...] = total.astype(jnp.bfloat16)
+
+    total = tsum[lax.div(hi, 2), parity].astype(jnp.float32)
+
+    @pl.when(far == 0)
+    def _():
+        remote(zfar, zfar, ts.at[1], tr.at[1], here).wait_recv()
+        out_ref[...] = (total + zpair[...].astype(jnp.float32) + zfar[...].astype(jnp.float32)).astype(jnp.bfloat16)
+
+    @pl.when(far == 1)
+    def _():
+        for k in range(3):
+            remote(zrecv.at[k], zrecv.at[k], zs.at[0], zr.at[k], here).wait_recv()
+        rest = sum(zrecv[k].astype(jnp.float32) for k in range(3))
+        out_ref[...] = (total + rest).astype(jnp.bfloat16)
 
     for copy in sends:
         copy.wait_send()
@@ -317,9 +429,17 @@
             def _():
                 y_copy(i, q).wait_send()
 
-            @pl.when((y == root(i)) & (hi != 2 * lo_of(i) + q))
-            def _():
-                z_copy(lo_of(i), q).wait_send()
+    for q in range(2):
+
+        @pl.when(hi != 2 * (1 - lo) + q)
+        def _():
+            z_copy(q).wait_send()
+
+    pair_copy().wait_send()
+
+    @pl.when(far == 1)
+    def _():
+        far_copy().wait_send()
 
     for d in (1, 2, 3):
         az_copy(d).wait_send()
@@ -368,8 +488,10 @@
             pltpu.VMEM((2, 3, 2, few, features), bf16),
             pltpu.VMEM((2, 2, few, features), bf16),
             pltpu.VMEM((3, few, features), bf16),
-            dma((4,)), dma((28,)), dma((NX, 2, 4)), dma((8, 2)), dma((8, 2)), dma((8, 2)), dma((2, 3, 2)),
-            dma((2, 2)), dma((3,)), dma((3,)), dma((3,)), dma((6,)), dma((3, 2)), dma((4,)), dma((4,)),
+            pltpu.VMEM((few, features), bf16),
+            pltpu.VMEM((few, features), bf16),
+            dma((4,)), dma((29,)), dma((NX, 2, 4)), dma((2,)), dma((8, 2)), dma((8, 2)), dma((8, 2)), dma((2, 3, 2)),
+            dma((2,)), dma((3,)), dma((2,)), dma((2,)), dma((3,)), dma((3,)), dma((6,)), dma((3, 2)), dma((4,)), dma((4,)),
         ],
         compiler_params=pltpu.CompilerParams(
             collective_id=0, has_side_effects=True, vmem_limit_bytes=48 * 1024 * 1024

time: 53.1 us -> 53 us (level)
  the two profiles are of different devices: /device:TPU:112 before, /device:TPU:36 now
where the time goes in v4:
time: 53 us; the launch traced here: 52.9 us
  Pallas kernels  51.6 us (97%)
  between operations  1.28 us (2%)
    pallas_call x1, Pallas kernels, shards(): pl.pallas_call(exchange_kernel, out_shape=(pltpu.VMEM((features, ff), f32...  48.7 us
    pallas_call x1, Pallas kernels, shards(): pl.pallas_call(store_kernel, out_shape=(jax.ShapeDtypeStruct((features, f...  2.92 us

profile of v4, /device:TPU:36, one launch (start us, length us, event | category | flops | bytes accessed | tf_op | source)
XLA Modules:
  0.0 52.9 jit_solution(16886101398537519653)
XLA Ops:
  1.3 48.7 %exchange.1 = (f32[1024,1664]{1,0:T(8,128)S(1)}, bf16[32,1024]{1,0:T(8,128)(2,1)S(1)}) custom-call(bf16[32,1024]{1,0:T(8,128)(2,1)} %act_hbm.1, bf16[1024,1664]{1,0:T(8,128)(2,1)} %weight_hbm.1, bf16[128,1664]{1,0:T(8,128)(2,1)} %grad_hbm.1, s32[1,128]{1,0:T(1,128)} %bitcast.1, s32[1]{0:T(128)S(6)} %copy.7.seed_ref), custom_call_target="tpu_custom_call" | custom-call | tf_op jit(solution)/shard_map/exchange/pallas_call | solution.py:472
  50.0 2.9 %store.1 = (f32[1024,1664]{1,0:T(8,128)}, bf16[32,1024]{1,0:T(8,128)(2,1)}) custom-call(f32[1024,1664]{1,0:T(8,128)S(1)} %get-tuple-element.4.total_ref, bf16[32,1024]{1,0:T(8,128)(2,1)S(1)} %get-tuple-element.5.rows_ref), custom_call_target="tpu_custom_call" | custom-call | tf_op jit(solution)/shard_map/store/pallas_call | solution.py:502

commit v5 on v4

--- a/solution.py
+++ b/solution.py
@@ -370,38 +370,43 @@
     @pl.when(core == 1)
     def _():
         send_core((FAR2, 1), (LEFT2, 1), (RIGHT2, 1))
-        add_cores((FAR2, 0), (LEFT2, 0), (RIGHT2, 0), (FAR2, 1))
-
-    add_plane(FAR, LEFT, RIGHT)
-    add_columns((OWN2, 0), (OWN2, 1))
+
     for d in range(4):
         ac_wait(d)
     turn_act(lo)
 
+    @pl.when(core == 1)
+    def _():
+        add_cores((FAR2, 0), (LEFT2, 0), (RIGHT2, 0), (FAR2, 1))
+
+    add_plane(FAR, LEFT, RIGHT)
+
     @pl.when(core == 0)
     def _():
         add_cores((FAR2, 1), (LEFT2, 1), (RIGHT2, 1))
 
+    accumulate(lo, spans[0], False)
+    add_columns((OWN2, 0), (OWN2, 1))
+
     @pl.when(core == 1)
     def _():
         add_columns((LEFT2, 1), (RIGHT2, 1))
 
-    accumulate(lo, spans[0], False)
     accumulate(lo, spans[1], False)
     add_columns((FAR2, 0), (LEFT2, 0), (RIGHT2, 0))
-    pass_on()
     for span in spans[2:]:
         accumulate(lo, span, False)
+
+    @pl.when(core == 0)
+    def _():
+        add_columns((FAR2, 1), (LEFT2, 1), (RIGHT2, 1))
+
+    @pl.when(core == 1)
+    def _():
+        add_columns((FAR2, 1))
+
+    pass_on()
     turn_act(1 - lo)
-
-    @pl.when(core == 0)
-    def _():
-        add_columns((FAR2, 1), (LEFT2, 1), (RIGHT2, 1))
-
-    @pl.when(core == 1)
-    def _():
-        add_columns((FAR2, 1))
-
     for span in spans:
         accumulate(1 - lo, span, True)
 

time: 53 us -> 52.4 us (0.989)
  the two profiles are of different devices: /device:TPU:36 before, /device:TPU:68 now
where the time goes in v5:
time: 52.4 us; the launch traced here: 52.2 us
  Pallas kernels  51 us (97%)
  between operations  1.28 us (2%)
    pallas_call x1, Pallas kernels, shards(): pl.pallas_call(exchange_kernel, out_shape=(pltpu.VMEM((features, ff), f32...  48 us
    pallas_call x1, Pallas kernels, shards(): pl.pallas_call(store_kernel, out_shape=(jax.ShapeDtypeStruct((features, f...  2.92 us

profile of v5, /device:TPU:68, one launch (start us, length us, event | category | flops | bytes accessed | tf_op | source)
XLA Modules:
  0.0 52.2 jit_solution(6842557034297011255)
XLA Ops:
  1.3 48.0 %exchange.1 = (f32[1024,1664]{1,0:T(8,128)S(1)}, bf16[32,1024]{1,0:T(8,128)(2,1)S(1)}) custom-call(bf16[32,1024]{1,0:T(8,128)(2,1)} %act_hbm.1, bf16[1024,1664]{1,0:T(8,128)(2,1)} %weight_hbm.1, bf16[128,1664]{1,0:T(8,128)(2,1)} %grad_hbm.1, s32[1,128]{1,0:T(1,128)} %bitcast.1, s32[1]{0:T(128)S(6)} %copy.7.seed_ref), custom_call_target="tpu_custom_call" | custom-call | tf_op jit(solution)/shard_map/exchange/pallas_call | solution.py:477
  49.3 2.9 %store.1 = (f32[1024,1664]{1,0:T(8,128)}, bf16[32,1024]{1,0:T(8,128)(2,1)}) custom-call(f32[1024,1664]{1,0:T(8,128)S(1)} %get-tuple-element.4.total_ref, bf16[32,1024]{1,0:T(8,128)(2,1)S(1)} %get-tuple-element.5.rows_ref), custom_call_target="tpu_custom_call" | custom-call | tf_op jit(solution)/shard_map/store/pallas_call | solution.py:507

commit v6 on v5

--- a/solution.py
+++ b/solution.py
@@ -255,13 +255,9 @@
     round_rows(1, 1)
     send_g(OWN, 1, left)
     round_rows(2, 2)
-    send_g(OWN, 3, pair)
-    send_g(OWN, 0, pair)
     for j, k in ((2, 3), (1, 0), (3, 2)):
         send_g(OWN, j, right)
         send_g(OWN, k, left)
-    send_g(OWN, 1, pair)
-    send_g(OWN, 2, pair)
     loads[3].wait()
 
     def turn_weight(n, _):
@@ -270,6 +266,8 @@
         return 0
 
     lax.fori_loop(0, features // 128, turn_weight, 0)
+    for j in (3, 0, 1, 2):
+        send_g(OWN, j, pair)
     project((OWN, 0, 4))
     send_core((OWN, 0), (OWN, 1))
     wait_g(LEFT, 0)
@@ -309,9 +307,11 @@
     add_cores((LEFT, 0), (LEFT, 1), (RIGHT, 0), (RIGHT, 1))
     wait_g(FAR, 2, 3)
     send_g(FAR, 2, pair)
+    project((FAR, 0, 4))
+    send_core((FAR, 0), (FAR, 1))
     wait_g(OWN2, 2)
-    project((FAR, 0, 4), (OWN2, 0, 4))
-    send_core((FAR, 0), (FAR, 1), (OWN2, 0), (OWN2, 1))
+    project((OWN2, 0, 4))
+    send_core((OWN2, 0), (OWN2, 1))
     wait_g(LEFT2, 3)
     send_half(LEFT2, 0, right)
     send_g(OWN2, 2, right)

time: 52.4 us -> 52.4 us (level)
  the two profiles are of different devices: /device:TPU:68 before, /device:TPU:69 now
where the time goes in v6:
time: 52.4 us; the launch traced here: 52.2 us
  Pallas kernels  51 us (97%)
  between operations  1.28 us (2%)
    pallas_call x1, Pallas kernels, shards(): pl.pallas_call(exchange_kernel, out_shape=(pltpu.VMEM((features, ff), f32...  48 us
    pallas_call x1, Pallas kernels, shards(): pl.pallas_call(store_kernel, out_shape=(jax.ShapeDtypeStruct((features, f...  2.92 us

profile of v6, /device:TPU:69, one launch (start us, length us, event | category | flops | bytes accessed | tf_op | source)
XLA Modules:
  0.0 52.2 jit_solution(230344821258930430)
XLA Ops:
  1.3 48.0 %exchange.1 = (f32[1024,1664]{1,0:T(8,128)S(1)}, bf16[32,1024]{1,0:T(8,128)(2,1)S(1)}) custom-call(bf16[32,1024]{1,0:T(8,128)(2,1)} %act_hbm.1, bf16[1024,1664]{1,0:T(8,128)(2,1)} %weight_hbm.1, bf16[128,1664]{1,0:T(8,128)(2,1)} %grad_hbm.1, s32[1,128]{1,0:T(1,128)} %bitcast.1, s32[1]{0:T(128)S(6)} %copy.7.seed_ref), custom_call_target="tpu_custom_call" | custom-call | tf_op jit(solution)/shard_map/exchange/pallas_call | solution.py:477
  49.3 2.9 %store.1 = (f32[1024,1664]{1,0:T(8,128)}, bf16[32,1024]{1,0:T(8,128)(2,1)}) custom-call(f32[1024,1664]{1,0:T(8,128)S(1)} %get-tuple-element.4.total_ref, bf16[32,1024]{1,0:T(8,128)(2,1)S(1)} %get-tuple-element.5.rows_ref), custom_call_target="tpu_custom_call" | custom-call | tf_op jit(solution)/shard_map/store/pallas_call | solution.py:507
